TPU v7x, 128 devices: a whole 4x4x4 slice. The times are simulated.
128 devices in a mesh: state: 2 (over x_lo), mode: 64 (over y, x_hi, z, core).
Axes of the slice: x: 4 (x_hi: 2, x_lo: 2; x = x_hi * 2 + x_lo), y: 4, z: 4, core: 2. Of those that a mesh axis runs over, the one named last changes fastest.
Arguments:
- core: bfloat16 [2, 512, 512, 256], P('state', 'mode'), may hold values from -6 to 6
- op_one: bfloat16 [2, 3, 512, 512], replicated, may hold values from -0.25 to 0.25
- op_two: bfloat16 [2, 3, 512, 512], replicated, may hold values from -0.25 to 0.25
- op_three: bfloat16 [2, 3, 256, 256], replicated, may hold values from -0.375 to 0.375
Outputs:
- relaxed: float32 [2, 512, 512, 256], P('state', 'mode')
All inputs are finite; a program needn't handle non-finite values.
Results may differ from a plain program's by a relative error of at most 0.0033.
Values may be sent and summed in bfloat16 or wider, within the bound.
No kernel may reach another device: no remote copies, remote signals or barrier semaphores. Data moves between devices by JAX's collectives and lax.ppermute only.
A program may use at most 64 MiB of HBM per device.

v0:
```python
import jax
import jax.numpy as jnp
from jax import lax
from jax.sharding import PartitionSpec as P


def swapped(block, axis, distance):
    count = lax.axis_size(axis)
    route = []
    for low in range(count):
        high = low | 1 << distance
        if high != low and high < count:
            route += [(low, high), (high, low)]
    return lax.ppermute(block, axis, route)


def mode_two_three(block, second, third):
    inner = jnp.einsum("ijk,lk->ijl", block, third, preferred_element_type=jnp.float32).astype(
        jnp.bfloat16
    )
    return jnp.einsum("ab,ibk->iak", second, inner, preferred_element_type=jnp.float32).astype(
        jnp.bfloat16
    )


def shards(core, op_one, op_two, op_three):
    own_core = core[0]
    term_count = op_one.shape[1]
    state_index = lax.axis_index("state")
    own_first = lax.dynamic_index_in_dim(op_one, state_index, 0, keepdims=False)
    own_second = lax.dynamic_index_in_dim(op_two, state_index, 0, keepdims=False)
    own_third = lax.dynamic_index_in_dim(op_three, state_index, 0, keepdims=False)
    sources = [own_core for term in range(term_count)]
    firsts = [own_first[term] for term in range(term_count)]
    seconds = [own_second[term] for term in range(term_count)]
    thirds = [own_third[term] for term in range(term_count)]
    prepared = [
        mode_two_three(sources[term], seconds[term], thirds[term]) for term in range(term_count)
    ]
    stacked = jnp.stack(prepared)
    first_stack = jnp.stack(firsts)
    pieces = lax.all_to_all(stacked, "mode", split_axis=2, concat_axis=1, tiled=True)
    diagonal_part = jnp.einsum(
        "rab,rbjk->ajk", first_stack[:2], pieces[:2], preferred_element_type=jnp.float32
    )
    coupling_part = jnp.einsum(
        "ab,bjk->ajk", first_stack[2], pieces[2], preferred_element_type=jnp.float32
    )
    combined = diagonal_part + swapped(coupling_part, "state", 0)
    applied = combined.astype(jnp.bfloat16)
    returned = lax.all_to_all(applied, "mode", split_axis=0, concat_axis=1, tiled=True)
    relaxed = own_core.astype(jnp.float32) - 0.5 * returned.astype(jnp.float32)
    return relaxed[None]


def solution(mesh):
    placed = (P("state", "mode", None, None), P(), P(), P())
    return jax.shard_map(
        shards,
        mesh=mesh,
        in_specs=placed,
        out_specs=P("state", "mode", None, None),
        check_vma=False,
    )
```

profile of v0, /device:TPU:1, one launch (start us, length us, event | category | flops | bytes accessed | tf_op | source)
XLA Modules:
  0.0 262.2 jit_solution(3244988878973622978)
XLA Ops:
  0.0 0.0 copy-start
  0.0 1.9 copy-done
  1.9 4.9 %convert_bitcast_fusion.2 = bf16[1,8,512,256]{2,3,1,0:T(8,128)(2,1)} fusion(bf16[1,8,512,256]{3,2,1,0:T(8,128)(2,1)} %param.4, bf16[2,3,512,512]{3,2,1,0:T(8,128)(2,1)S(1)} %copy-done, s32[]{:T(128)S(6)} %select_n.7, bf16[2,3,256,256]{3,2,1,0:T(8,128)(2,1)} %param.7), kind=kOutput, calls=%fused_computation.28 | convolution fusion | flops 1612709888 | bytes 4850688 | tf_op jit(solution)/shard_map/ab,ibk->iak/dot_general | solution.py:21
  6.8 4.9 %convert_bitcast_fusion.1 = bf16[1,8,512,256]{2,3,1,0:T(8,128)(2,1)} fusion(bf16[1,8,512,256]{3,2,1,0:T(8,128)(2,1)} %param.4, bf16[2,3,512,512]{3,2,1,0:T(8,128)(2,1)S(1)} %copy-done, s32[]{:T(128)S(6)} %select_n.7, s32[]{:T(128)S(6)} %add.12, bf16[2,3,256,256]{3,2,1,0:T(8,128)(2,1)} %param.7), kind=kOutput, calls=%fused_computation.26 | convolution fusion | flops 1612709888 | bytes 4851712 | tf_op jit(solution)/shard_map/ab,ibk->iak/dot_general | solution.py:21
  11.6 4.8 %convert_bitcast_fusion = bf16[1,8,512,256]{2,3,1,0:T(8,128)(2,1)} fusion(bf16[1,8,512,256]{3,2,1,0:T(8,128)(2,1)} %param.4, bf16[2,3,512,512]{3,2,1,0:T(8,128)(2,1)S(1)} %copy-done, s32[]{:T(128)S(6)} %select_n.7, s32[]{:T(128)S(6)} %add.15, bf16[2,3,256,256]{3,2,1,0:T(8,128)(2,1)} %param.7), kind=kOutput, calls=%fused_computation.24 | convolution fusion | flops 1612709888 | bytes 4851712 | tf_op jit(solution)/shard_map/ab,ibk->iak/dot_general | solution.py:21
  16.4 6.4 %pad_maximum_fusion = bf16[3,8,512,256]{2,3,1,0:T(8,128)(2,1)} fusion(bf16[1,8,512,256]{2,3,1,0:T(8,128)(2,1)} %convert_bitcast_fusion, bf16[1,8,512,256]{2,3,1,0:T(8,128)(2,1)} %convert_bitcast_fusion.1, bf16[1,8,512,256]{2,3,1,0:T(8,128)(2,1)} %convert_bitcast_fusion.2), kind=kLoop, calls=%fused_computation | loop fusion | flops 6291456 | bytes 12582912 | tf_op jit(solution)/shard_map/stack | solution.py:40
  22.9 9.3 %copy.12 = bf16[3,8,512,256]{3,1,0,2:T(8,128)(2,1)} copy(bf16[3,8,512,256]{2,3,1,0:T(8,128)(2,1)} %pad_maximum_fusion) | data formatting | bytes 12582912 | tf_op jit(solution)/shard_map/stack | solution.py:40
  32.2 87.9 %all_to_all.24 = bf16[3,8,512,256]{3,1,0,2:T(8,128)(2,1)S(1)} all-to-all(bf16[3,8,512,256]{3,1,0,2:T(8,128)(2,1)} %copy.12), channel_id=1, replica_groups=mesh['state'=2,'mode'=64] {'mode'}, dimensions={2} | all-to-all | bytes 12582912 | tf_op jit(solution)/shard_map/all_to_all | solution.py:42
  120.0 1.5 copy.31
  121.5 0.0 copy-start.3
  121.5 0.1 slice.65
  121.7 1.7 copy-done.3
  123.4 1.7 fusion.4
  125.1 0.7 collective-permute-start
  125.8 0.1 dynamic-slice_bitcast_fusion.9
  125.9 0.3 slice.64
  126.2 91.3 %collective-permute-done = f32[512,8,256]{2,0,1:T(8,128)S(1)} collective-permute-done((f32[512,8,256]{2,0,1:T(8,128)S(1)}, f32[512,8,256]{2,0,1:T(8,128)S(1)}, u32[]{:S(2)}, u32[]{:S(2)}) %collective-permute-start) | collective-permute-done | bytes 4194336 | tf_op jit(solution)/shard_map/ppermute | solution.py:14
  217.4 3.0 %fusion = bf16[512,8,256]{2,0,1:T(8,128)(2,1)S(1)} fusion(f32[512,8,256]{2,0,1:T(8,128)S(1)} %collective-permute-done, bf16[2,64,8,8,256]{4,3,1,2,0:T(8,128)(2,1)S(1)} %slice.64, bf16[1,512,512]{2,1,0:T(8,128)(2,1)S(1)} %get-tuple-element.6, bf16[1,512,512]{2,1,0:T(8,128)(2,1)S(1)} %get-tuple-element.5), kind=kOutput, calls=%fused_computation.4 | convolution fusion | flops 2151677952 | bytes 11534336 | tf_op jit(solution)/shard_map/rab,rbjk->ajk/dot_general | solution.py:43
  220.4 1.2 copy.16
  221.6 36.6 %all_to_all.25 = bf16[512,8,256]{2,1,0:T(8,128)(2,1)S(1)} all-to-all(bf16[512,8,256]{2,1,0:T(8,128)(2,1)S(1)} %copy.16), channel_id=1, replica_groups=mesh['state'=2,'mode'=64] {'mode'}, dimensions={0} | all-to-all | bytes 4194304 | tf_op jit(solution)/shard_map/all_to_all | solution.py:51
  258.2 0.0 copy-start.2
  258.2 0.3 convert_multiply_fusion
  258.5 0.0 copy-start.1
  258.5 1.3 copy-done.2
  259.8 2.5 bitcast_subtract_fusion
  262.2 0.0 copy-done.1
Async XLA Ops:
  0.0 1.9 copy-start
  121.5 1.9 copy-start.3
  125.1 92.3 %collective-permute-start = (f32[512,8,256]{2,0,1:T(8,128)S(1)}, f32[512,8,256]{2,0,1:T(8,128)S(1)}, u32[]{:S(2)}, u32[]{:S(2)}) collective-permute-start(f32[512,8,256]{2,0,1:T(8,128)S(1)} %fusion.4), channel_id=1, source_target_pairs={{0,64},{64,0},{1,65},{65,1},{2,66},{66,2},{3,67},{67,3},{4,68},{68... | collective-permute-start | bytes 12582920 | tf_op jit(solution)/shard_map/ppermute | solution.py:14
  258.2 1.6 copy-start.2
  258.5 3.8 %copy-start.1 = (bf16[2,3,512,512]{3,2,1,0:T(8,128)(2,1)S(1)}, bf16[2,3,512,512]{3,2,1,0:T(8,128)(2,1)}, u32[]{:S(2)}) copy-start(bf16[2,3,512,512]{3,2,1,0:T(8,128)(2,1)} %param.6) | copy-start | bytes 9437188
where the time goes:
time: 263 us; the launch traced here: 262 us
  blocking collectives  124 us (47%)
  waiting for transfers between devices  91.3 us (35%)
  matrix products  19.2 us (7%)
  local copies, waits for them, and re-layouts  17.3 us (7%)
  other arithmetic  9.17 us (3%)
    ppermute x1, waiting for transfers between devices, swapped(): return lax.ppermute(block, axis, route)  91.3 us
    all_to_all x1, blocking collectives, shards(): lax.all_to_all(stacked, 'mode', split_axis=2, concat_axis=1, tiled=True)  87.9 us
    all_to_all x1, blocking collectives, shards(): lax.all_to_all(applied, 'mode', split_axis=0, concat_axis=1, tiled=True)  36.6 us
    dot_general x3, matrix products, mode_two_three(): jnp.einsum('ab,ibk->iak', second, inner, preferred_element_type=jnp.float32)  14.5 us
    another operation x1, local copies, waits for them, and re-layouts, shards(): stacked = jnp.stack(prepared)  9.27 us
    another operation x1, other arithmetic, shards(): stacked = jnp.stack(prepared)  6.45 us
  transfers between devices with their start and end apart: 1, of which 1 were waited for; matrix products, arithmetic and copies ran while one was open for 0% of the time, Pallas kernels for 0%

commit v1 on v0

v1 whole, which is shorter than its diff:
```python
import jax
import jax.numpy as jnp
from jax import lax
from jax.sharding import PartitionSpec as P

EVERY = ("state", "mode")


def shards(core, op_one, op_two, op_three):
    own_core = core[0]
    rows, second_extent, third_extent = own_core.shape
    states, terms, first_extent, _ = op_one.shape
    owners = first_extent // rows
    columns = second_extent // (states * owners)
    state_index = lax.axis_index("state")
    own_second = lax.dynamic_index_in_dim(op_two, state_index, 0, keepdims=False)
    own_third = lax.dynamic_index_in_dim(op_three, state_index, 0, keepdims=False)
    prepared = []
    for term in range(terms):
        inner = jnp.einsum(
            "ijk,lk->jil", own_core, own_third[term], preferred_element_type=jnp.float32
        ).astype(jnp.bfloat16)
        prepared.append(
            jnp.einsum(
                "ab,bik->aik", own_second[term], inner, preferred_element_type=jnp.float32
            ).astype(jnp.bfloat16)
        )
    pieces = [
        lax.all_to_all(value, EVERY, split_axis=0, concat_axis=0, tiled=True).reshape(
            states, owners, columns, rows, third_extent
        )
        for value in prepared
    ]
    pieces = [
        value.transpose(0, 1, 3, 2, 4).reshape(states, first_extent, columns, third_extent)
        for value in pieces
    ]
    applied = []
    for state in range(states):
        sources = [(state, 0), (state, 1), (1 - state, 2)]
        total = sum(
            jnp.einsum(
                "ab,bjk->ajk",
                op_one[source, term],
                pieces[term][source],
                preferred_element_type=jnp.float32,
            )
            for source, term in sources
        )
        applied.append(total.astype(jnp.bfloat16))
    sent = jnp.stack(applied).reshape(states, owners, rows, columns, third_extent)
    sent = sent.transpose(0, 1, 3, 2, 4).reshape(second_extent, rows, third_extent)
    returned = lax.all_to_all(sent, EVERY, split_axis=0, concat_axis=0, tiled=True)
    returned = returned.reshape(second_extent, rows, third_extent)
    relaxed = own_core.astype(jnp.float32) - 0.5 * returned.transpose(1, 0, 2).astype(jnp.float32)
    return relaxed[None]


def solution(mesh):
    placed = (P("state", "mode", None, None), P(), P(), P())
    return jax.shard_map(
        shards,
        mesh=mesh,
        in_specs=placed,
        out_specs=P("state", "mode", None, None),
        check_vma=False,
    )
```

time: 263 us -> 184 us (0.70)
  blocking collectives: 124 us -> 34.7 us
  waiting for transfers between devices: 91.3 us -> 66.7 us
  starting transfers between devices: 0.71 us -> 21.9 us
  local copies, waits for them, and re-layouts: 17.3 us -> 31.7 us
  other arithmetic: 9.17 us -> 3.13 us
  matrix products: 19.2 us -> 24.6 us
    ppermute x1 -> x0, waiting for transfers between devices: 91.3 us -> none  [swapped(): return lax.ppermute(block, axis, route)]
    all_to_all x2 -> x1, blocking collectives: 124 us -> 34.7 us  [shards(): lax.all_to_all(sent, EVERY, split_axis=0, concat_axis=0, tiled=True)]
    all_to_all x0 -> x3, waiting for transfers between devices: none -> 66.7 us  [shards(): lax.all_to_all(value, EVERY, split_axis=0, concat_axis=0, tiled=True)]
    all_to_all x0 -> x3, starting transfers between devices: none -> 21.9 us  [shards(): lax.all_to_all(value, EVERY, split_axis=0, concat_axis=0, tiled=True)]
    convert_element_type x1 -> x5, local copies, waits for them, and re-layouts: 1.18 us -> 16.8 us  [the longest x3 12.3 us: shards(): prepared.append(jnp.einsum('ab,bik->aik', own_second[term], inner, prefer...]
    another operation x1 -> x0, local copies, waits for them, and re-layouts: 9.27 us -> none  [shards(): stacked = jnp.stack(prepared)]
    slice x3, local copies, waits for them, and re-layouts: 0.5 us -> 8.97 us  [shards(): pieces[term][source]]
    another operation x1 -> x0, other arithmetic: 6.45 us -> none  [shards(): stacked = jnp.stack(prepared)]
  transfers between devices with their start and end apart: 1 -> 3, of which waited for: 1 -> 3; matrix products, arithmetic and copies ran while one was open for 0% -> 13% of each run, Pallas kernels for 0% -> 0%
where the time goes in v1:
time: 184 us; the launch traced here: 183 us
  waiting for transfers between devices  66.7 us (36%)
  blocking collectives  34.7 us (19%)
  local copies, waits for them, and re-layouts  31.7 us (17%)
  matrix products  24.6 us (13%)
  starting transfers between devices  21.9 us (12%)
  other arithmetic  3.13 us (2%)
    all_to_all x3, waiting for transfers between devices, shards(): lax.all_to_all(value, EVERY, split_axis=0, concat_axis=0, tiled=True)  66.7 us
    all_to_all x1, blocking collectives, shards(): lax.all_to_all(sent, EVERY, split_axis=0, concat_axis=0, tiled=True)  34.7 us
    all_to_all x3, starting transfers between devices, shards(): lax.all_to_all(value, EVERY, split_axis=0, concat_axis=0, tiled=True)  21.9 us
    dot_general x3, matrix products, shards(): jnp.einsum('ab,bik->aik', own_second[term], inner, preferred_element_type...  14.5 us
    convert_element_type x3, local copies, waits for them, and re-layouts, shards(): prepared.append(jnp.einsum('ab,bik->aik', own_second[term], inner, prefer...  12.3 us
    dot_general x6, matrix products, shards(): jnp.einsum('ab,bjk->ajk', op_one[source, term], pieces[term][source], pre...  10.1 us
    slice x3, local copies, waits for them, and re-layouts, shards(): pieces[term][source]  8.97 us
    convert_element_type x2, local copies, waits for them, and re-layouts, shards(): applied.append(total.astype(jnp.bfloat16))  4.54 us
  transfers between devices with their start and end apart: 3, of which 3 were waited for; matrix products, arithmetic and copies ran while one was open for 13% of the time, Pallas kernels for 0%

profile of v1, /device:TPU:1, one launch (start us, length us, event | category | flops | bytes accessed | tf_op | source)
XLA Modules:
  0.0 182.9 jit_solution(12865789251767898271)
XLA Ops:
  0.0 0.0 copy-start
  0.0 1.9 %copy-done = bf16[2,3,512,512]{3,2,1,0:T(8,128)(2,1)S(1)} copy-done((bf16[2,3,512,512]{3,2,1,0:T(8,128)(2,1)S(1)}, bf16[2,3,512,512]{3,2,1,0:T(8,128)(2,1)}, u32[]{:S(2)}) %copy-start) | copy-done | bytes 3145752
  1.9 4.8 %fusion.33 = bf16[512,8,256]{2,0,1:T(8,128)(2,1)} fusion(bf16[1,8,512,256]{3,2,1,0:T(8,128)(2,1)} %param.4, bf16[2,3,512,512]{3,2,1,0:T(8,128)(2,1)S(1)} %copy-done, s32[]{:T(128)S(6)} %select_n.6, s32[]{:T(128)S(6)} %add.27, bf16[2,3,256,256]{3,2,1,0:T(8,128)(2,1)} %param.7), kind=kOutput, calls=%fused_computation.21 | convolution fusion | flops 1612709888 | bytes 4851712 | tf_op jit(solution)/shard_map/ab,bik->aik/dot_general | solution.py:24
  6.7 4.1 %copy.71 = bf16[512,8,256]{2,1,0:T(8,128)(2,1)} copy(bf16[512,8,256]{2,0,1:T(8,128)(2,1)} %fusion.33) | data formatting | bytes 4194304 | tf_op jit(solution)/shard_map/convert_element_type | solution.py:26
  10.8 11.9 %all-to-all-start.1 = ((bf16[512,8,256]{2,1,0:T(8,128)(2,1)}), bf16[512,8,256]{2,1,0:T(8,128)(2,1)}, u32[]{:S(2)}, u32[]{:S(2)}) async-start(bf16[512,8,256]{2,1,0:T(8,128)(2,1)} %copy.71), calls=%async_computation.1 | async-start | bytes 4194304 | tf_op jit(solution)/shard_map/all_to_all | solution.py:29
  22.7 4.8 %fusion.38 = bf16[512,8,256]{2,0,1:T(8,128)(2,1)} fusion(bf16[1,8,512,256]{3,2,1,0:T(8,128)(2,1)} %param.4, bf16[2,3,512,512]{3,2,1,0:T(8,128)(2,1)S(1)} %copy-done, s32[]{:T(128)S(6)} %select_n.6, s32[]{:T(128)S(6)} %add.29, bf16[2,3,256,256]{3,2,1,0:T(8,128)(2,1)} %param.7), kind=kOutput, calls=%fused_computation.22 | convolution fusion | flops 1612709888 | bytes 4851712 | tf_op jit(solution)/shard_map/ab,bik->aik/dot_general | solution.py:24
  27.6 4.1 %copy.76 = bf16[512,8,256]{2,1,0:T(8,128)(2,1)} copy(bf16[512,8,256]{2,0,1:T(8,128)(2,1)} %fusion.38) | data formatting | bytes 4194304 | tf_op jit(solution)/shard_map/convert_element_type | solution.py:26
  31.7 21.2 %all-to-all-done.1 = bf16[512,8,256]{2,1,0:T(8,128)(2,1)} async-done(((bf16[512,8,256]{2,1,0:T(8,128)(2,1)}), bf16[512,8,256]{2,1,0:T(8,128)(2,1)}, u32[]{:S(2)}, u32[]{:S(2)}) %all-to-all-start.1) | async-done | bytes 2097184 | tf_op jit(solution)/shard_map/all_to_all | solution.py:29
  52.9 5.0 %all-to-all-start.2 = ((bf16[512,8,256]{2,1,0:T(8,128)(2,1)}), bf16[512,8,256]{2,1,0:T(8,128)(2,1)}, u32[]{:S(2)}, u32[]{:S(2)}) async-start(bf16[512,8,256]{2,1,0:T(8,128)(2,1)} %copy.76), calls=%async_computation.2 | async-start | bytes 4194304 | tf_op jit(solution)/shard_map/all_to_all | solution.py:29
  57.9 4.8 %fusion.28 = bf16[512,8,256]{2,0,1:T(8,128)(2,1)} fusion(bf16[1,8,512,256]{3,2,1,0:T(8,128)(2,1)} %param.4, bf16[2,3,512,512]{3,2,1,0:T(8,128)(2,1)S(1)} %copy-done, s32[]{:T(128)S(6)} %select_n.6, bf16[2,3,256,256]{3,2,1,0:T(8,128)(2,1)} %param.7), kind=kOutput, calls=%fused_computation.20 | convolution fusion | flops 1612709888 | bytes 4850688 | tf_op jit(solution)/shard_map/ab,bik->aik/dot_general | solution.py:24
  62.7 4.1 %copy.66 = bf16[512,8,256]{2,1,0:T(8,128)(2,1)} copy(bf16[512,8,256]{2,0,1:T(8,128)(2,1)} %fusion.28) | data formatting | bytes 4194304 | tf_op jit(solution)/shard_map/convert_element_type | solution.py:26
  66.8 21.4 %all-to-all-done.2 = bf16[512,8,256]{2,1,0:T(8,128)(2,1)} async-done(((bf16[512,8,256]{2,1,0:T(8,128)(2,1)}), bf16[512,8,256]{2,1,0:T(8,128)(2,1)}, u32[]{:S(2)}, u32[]{:S(2)}) %all-to-all-start.2) | async-done | bytes 2097184 | tf_op jit(solution)/shard_map/all_to_all | solution.py:29
  88.2 5.0 %all-to-all-start = ((bf16[512,8,256]{2,1,0:T(8,128)(2,1)}), bf16[512,8,256]{2,1,0:T(8,128)(2,1)}, u32[]{:S(2)}, u32[]{:S(2)}) async-start(bf16[512,8,256]{2,1,0:T(8,128)(2,1)} %copy.66), calls=%async_computation | async-start | bytes 4194304 | tf_op jit(solution)/shard_map/all_to_all | solution.py:29
  93.2 3.1 %fusion.80 = (bf16[1,64,8,4,256]{4,2,3,1,0:T(8,128)(2,1)}, bf16[1,64,8,4,256]{4,2,3,1,0:T(8,128)(2,1)}) fusion(bf16[2,64,8,4,256]{4,2,3,1,0:T(8,128)(2,1)} %bitcast.19), kind=kLoop, calls=%fused_computation.63 | loop fusion | bytes 4194304 | tf_op jit(solution)/shard_map/slice | solution.py:45
  96.3 3.0 %fusion.79 = (bf16[1,64,8,4,256]{4,2,3,1,0:T(8,128)(2,1)}, bf16[1,64,8,4,256]{4,2,3,1,0:T(8,128)(2,1)}) fusion(bf16[2,64,8,4,256]{4,2,3,1,0:T(8,128)(2,1)} %bitcast.30), kind=kLoop, calls=%fused_computation.62 | loop fusion | bytes 4194304 | tf_op jit(solution)/shard_map/slice | solution.py:45
  99.3 24.1 %all-to-all-done = bf16[512,8,256]{2,1,0:T(8,128)(2,1)} async-done(((bf16[512,8,256]{2,1,0:T(8,128)(2,1)}), bf16[512,8,256]{2,1,0:T(8,128)(2,1)}, u32[]{:S(2)}, u32[]{:S(2)}) %all-to-all-start) | async-done | bytes 2097184 | tf_op jit(solution)/shard_map/all_to_all | solution.py:29
  123.5 0.0 copy-start.2
  123.5 0.0 copy-start.5
  123.5 2.8 %fusion.81 = (bf16[1,64,8,4,256]{4,2,3,1,0:T(8,128)(2,1)S(1)}, bf16[1,64,8,4,256]{4,2,3,1,0:T(8,128)(2,1)}) fusion(bf16[2,64,8,4,256]{4,2,3,1,0:T(8,128)(2,1)} %bitcast.8), kind=kLoop, calls=%fused_computation.64 | loop fusion | bytes 4194304 | tf_op jit(solution)/shard_map/slice | solution.py:45
  126.3 0.0 copy-done.2
  126.3 0.0 copy-done.5
  126.3 0.8 fusion.51
  127.1 0.0 copy-start.4
  127.1 0.8 fusion.53
  127.9 0.5 copy-done.4
  128.3 1.7 fusion.43
  130.0 2.3 %copy.79 = bf16[512,4,256]{2,0,1:T(8,128)(2,1)} copy(bf16[512,4,256]{0,2,1:T(8,128)(2,1)} %fusion.43) | data formatting | bytes 2097152 | tf_op jit(solution)/shard_map/convert_element_type | solution.py:50
  132.3 0.0 copy-start.1
  132.3 2.2 %fusion.48 = f32[4,256,512]{2,1,0:T(8,128)S(1)} fusion(bf16[1,64,8,4,256]{4,2,3,1,0:T(8,128)(2,1)} %get-tuple-element.10, bf16[2,3,512,512]{3,2,1,0:T(8,128)(2,1)} %param.5), kind=kOutput, calls=%fused_computation.28 | convolution fusion | flops 536870912 | bytes 3670016 | tf_op jit(solution)/shard_map/ab,bjk->ajk/dot_general | solution.py:42
  134.5 0.0 copy-start.3
  134.5 0.0 copy-done.1
  134.6 1.9 %fusion.46 = f32[4,256,512]{2,1,0:T(8,128)S(1)} fusion(bf16[1,64,8,4,256]{4,2,3,1,0:T(8,128)(2,1)S(1)} %copy-done.1, bf16[2,3,512,512]{3,2,1,0:T(8,128)(2,1)} %param.5), kind=kOutput, calls=%fused_computation.26 | convolution fusion | flops 536870912 | bytes 3670016 | tf_op jit(solution)/shard_map/ab,bjk->ajk/dot_general | solution.py:42
  136.4 0.0 copy-done.3
  136.5 2.8 %fusion.44 = bf16[512,4,256]{0,2,1:T(8,128)(2,1)} fusion(f32[4,256,512]{2,1,0:T(8,128)S(1)} %fusion.48, f32[4,256,512]{2,1,0:T(8,128)S(1)} %fusion.46, bf16[1,64,8,4,256]{4,2,3,1,0:T(8,128)(2,1)S(1)} %copy-done.3, bf16[2,3,512,512]{3,2,1,0:T(8,128)(2,1)} %param.5), kind=kOutput, calls=%fused_computation.24 | convolution fusion | flops 538443776 | bytes 6815744 | tf_op jit(solution)/shard_map/ab,bjk->ajk/dot_general | solution.py:42
  139.2 2.3 %copy.86 = bf16[512,4,256]{2,0,1:T(8,128)(2,1)} copy(bf16[512,4,256]{0,2,1:T(8,128)(2,1)} %fusion.44) | data formatting | bytes 2097152 | tf_op jit(solution)/shard_map/convert_element_type | solution.py:50
  141.5 1.7 maximum_bitcast_fusion
  143.2 0.3 copy.87
  143.5 0.0 copy-start.6
  143.5 34.7 %all_to_all.20 = bf16[512,8,256]{2,1,0:T(8,128)(2,1)S(1)} all-to-all(bf16[512,8,256]{2,1,0:T(8,128)(2,1)S(1)} %bitcast.149), channel_id=1, replica_groups=mesh['state'=2,'mode'=64] {'state','mode'}, dimensions={0} | all-to-all | bytes 4194304 | tf_op jit(solution)/shard_map/all_to_all | solution.py:53
  178.2 0.0 copy-done.6
  178.2 1.4 fusion
  179.6 3.3 %copy.88 = f32[1,8,512,256]{3,2,1,0:T(8,128)} copy(f32[1,8,512,256]{3,1,2,0:T(8,128)S(1)} %fusion) | data formatting | bytes 8388608 | tf_op jit(solution)/shard_map/broadcast_in_dim | solution.py:56
Async XLA Ops:
  0.0 1.9 %copy-start = (bf16[2,3,512,512]{3,2,1,0:T(8,128)(2,1)S(1)}, bf16[2,3,512,512]{3,2,1,0:T(8,128)(2,1)}, u32[]{:S(2)}) copy-start(bf16[2,3,512,512]{3,2,1,0:T(8,128)(2,1)} %param.6) | copy-start | bytes 9437188
  10.8 42.1 %all-to-all-start.1 = ((bf16[512,8,256]{2,1,0:T(8,128)(2,1)}), bf16[512,8,256]{2,1,0:T(8,128)(2,1)}, u32[]{:S(2)}, u32[]{:S(2)}) async-start(bf16[512,8,256]{2,1,0:T(8,128)(2,1)} %copy.71), calls=%async_computation.1 | async-start | bytes 4194304 | tf_op jit(solution)/shard_map/all_to_all | solution.py:29
  52.9 35.3 %all-to-all-start.2 = ((bf16[512,8,256]{2,1,0:T(8,128)(2,1)}), bf16[512,8,256]{2,1,0:T(8,128)(2,1)}, u32[]{:S(2)}, u32[]{:S(2)}) async-start(bf16[512,8,256]{2,1,0:T(8,128)(2,1)} %copy.76), calls=%async_computation.2 | async-start | bytes 4194304 | tf_op jit(solution)/shard_map/all_to_all | solution.py:29
  88.2 35.3 %all-to-all-start = ((bf16[512,8,256]{2,1,0:T(8,128)(2,1)}), bf16[512,8,256]{2,1,0:T(8,128)(2,1)}, u32[]{:S(2)}, u32[]{:S(2)}) async-start(bf16[512,8,256]{2,1,0:T(8,128)(2,1)} %copy.66), calls=%async_computation | async-start | bytes 4194304 | tf_op jit(solution)/shard_map/all_to_all | solution.py:29
  123.5 2.8 %copy-start.2 = (bf16[1,64,8,4,256]{4,2,3,1,0:T(8,128)(2,1)S(1)}, bf16[1,64,8,4,256]{4,2,3,1,0:T(8,128)(2,1)}, u32[]{:S(2)}) copy-start(bf16[1,64,8,4,256]{4,2,3,1,0:T(8,128)(2,1)} %get-tuple-element.7) | copy-start | bytes 3145732
  123.5 2.8 %copy-start.5 = (bf16[2,3,512,512]{3,2,1,0:T(8,128)(2,1)S(1)}, bf16[2,3,512,512]{3,2,1,0:T(8,128)(2,1)}, u32[]{:S(2)}) copy-start(bf16[2,3,512,512]{3,2,1,0:T(8,128)(2,1)} %param.5) | copy-start | bytes 9437188
  127.1 1.2 copy-start.4
  132.3 2.2 %copy-start.1 = (bf16[1,64,8,4,256]{4,2,3,1,0:T(8,128)(2,1)S(1)}, bf16[1,64,8,4,256]{4,2,3,1,0:T(8,128)(2,1)}, u32[]{:S(2)}) copy-start(bf16[1,64,8,4,256]{4,2,3,1,0:T(8,128)(2,1)} %get-tuple-element.8) | copy-start | bytes 3145732
  134.5 1.9 %copy-start.3 = (bf16[1,64,8,4,256]{4,2,3,1,0:T(8,128)(2,1)S(1)}, bf16[1,64,8,4,256]{4,2,3,1,0:T(8,128)(2,1)}, u32[]{:S(2)}) copy-start(bf16[1,64,8,4,256]{4,2,3,1,0:T(8,128)(2,1)} %get-tuple-element.6) | copy-start | bytes 3145732
  143.5 34.7 %copy-start.6 = (bf16[1,8,512,256]{3,2,1,0:T(8,128)(2,1)S(1)}, bf16[1,8,512,256]{3,2,1,0:T(8,128)(2,1)}, u32[]{:S(2)}) copy-start(bf16[1,8,512,256]{3,2,1,0:T(8,128)(2,1)} %param.4) | copy-start | bytes 6291460

commit v2 on v1

v2 whole, which is shorter than its diff:
```python
import jax
import jax.numpy as jnp
from jax import lax
from jax.experimental import pallas as pl
from jax.experimental.pallas import tpu as pltpu
from jax.sharding import PartitionSpec as P

EVERY = ("state", "mode")
LANES = 128


def prepare(state_ref, core_ref, second_ref, third_ref, sent_ref, rows_ref):
    rows, second_extent, third_extent = core_ref.shape
    second = second_ref[0, 0]
    third = third_ref[0, 0]

    def one_row(row, carry):
        inner = lax.dot_general(
            core_ref[row],
            third,
            (((1,), (1,)), ((), ())),
            preferred_element_type=jnp.float32,
        ).astype(jnp.bfloat16)
        value = jnp.dot(second, inner, preferred_element_type=jnp.float32)
        for part in range(third_extent // LANES):
            rows_ref[part, pl.ds(row, second_extent, stride=rows), :] = value[
                :, part * LANES : (part + 1) * LANES
            ]
        return carry

    lax.fori_loop(0, rows, one_row, 0)
    for part in range(third_extent // LANES):
        sent_ref[:, 0, :, part * LANES : (part + 1) * LANES] = (
            rows_ref[part].astype(jnp.bfloat16).reshape(*sent_ref.shape[:1], sent_ref.shape[2], LANES)
        )


def apply_first(first_ref, got_ref, sent_ref):
    states, _, first_extent, _ = first_ref.shape
    devices, terms, held, third_extent = got_ref.shape
    owners = devices // states
    rows = first_extent // owners

    def piece(source, term, column):
        value = got_ref[
            source * owners : (source + 1) * owners, term, column * rows : (column + 1) * rows
        ]
        return (
            value.astype(jnp.float32).reshape(first_extent, third_extent).astype(jnp.bfloat16)
        )

    for column in range(held // rows):
        for state in range(states):
            total = jnp.zeros((first_extent, third_extent), jnp.float32)
            for source, term in ((state, 0), (state, 1), (1 - state, 2)):
                total += jnp.dot(
                    first_ref[source, term],
                    piece(source, term, column),
                    preferred_element_type=jnp.float32,
                )
            sent_ref[
                state * owners : (state + 1) * owners, column * rows : (column + 1) * rows
            ] = total.reshape(owners, rows, third_extent).astype(jnp.bfloat16)


def relax(got_ref, core_ref, relaxed_ref, rows_ref):
    row = pl.program_id(0)
    rows = pl.num_programs(0)

    @pl.when(row == 0)
    def _():
        for part in range(rows_ref.shape[0]):
            rows_ref[part] = (
                got_ref[:, :, part * LANES : (part + 1) * LANES]
                .astype(jnp.float32)
                .reshape(rows_ref.shape[1:])
            )

    for part in range(rows_ref.shape[0]):
        lanes = slice(part * LANES, (part + 1) * LANES)
        applied = rows_ref[part, pl.ds(row, core_ref.shape[1], stride=rows), :]
        relaxed_ref[0, :, lanes] = core_ref[0, :, lanes].astype(jnp.float32) - 0.5 * applied


def shards(core, op_one, op_two, op_three):
    own_core = core[0]
    rows, second_extent, third_extent = own_core.shape
    states, terms, first_extent, _ = op_one.shape
    devices = states * (first_extent // rows)
    held = second_extent // devices * rows
    state_index = lax.axis_index("state").astype(jnp.int32).reshape(1)
    whole = pl.BlockSpec(memory_space=pltpu.VMEM)

    sent = pl.pallas_call(
        prepare,
        grid_spec=pltpu.PrefetchScalarGridSpec(
            num_scalar_prefetch=1,
            grid=(terms,),
            in_specs=[
                pl.BlockSpec((rows, second_extent, third_extent), lambda term, state: (0, 0, 0)),
                pl.BlockSpec(
                    (1, 1, second_extent, second_extent), lambda term, state: (state[0], term, 0, 0)
                ),
                pl.BlockSpec(
                    (1, 1, third_extent, third_extent), lambda term, state: (state[0], term, 0, 0)
                ),
            ],
            out_specs=pl.BlockSpec(
                (devices, 1, held, third_extent), lambda term, state: (0, term, 0, 0)
            ),
            scratch_shapes=[pltpu.VMEM((third_extent // LANES, rows * second_extent, LANES), jnp.float32)],
        ),
        out_shape=jax.ShapeDtypeStruct((devices, terms, held, third_extent), jnp.bfloat16),
        name="prepare",
    )(state_index, own_core, op_two, op_three)
    got = lax.all_to_all(sent, EVERY, split_axis=0, concat_axis=0, tiled=True)
    applied = pl.pallas_call(
        apply_first,
        in_specs=[whole, whole],
        out_specs=whole,
        out_shape=jax.ShapeDtypeStruct((devices, held, third_extent), jnp.bfloat16),
        name="apply_first",
    )(op_one, got)
    returned = lax.all_to_all(applied, EVERY, split_axis=0, concat_axis=0, tiled=True)
    relaxed = pl.pallas_call(
        relax,
        grid=(rows,),
        in_specs=[
            pl.BlockSpec((devices, held, third_extent), lambda row: (0, 0, 0)),
            pl.BlockSpec((1, second_extent, third_extent), lambda row: (row, 0, 0)),
        ],
        out_specs=pl.BlockSpec((1, second_extent, third_extent), lambda row: (row, 0, 0)),
        scratch_shapes=[pltpu.VMEM((third_extent // LANES, rows * second_extent, LANES), jnp.float32)],
        out_shape=jax.ShapeDtypeStruct(own_core.shape, jnp.float32),
        name="relax",
    )(returned, own_core)
    return relaxed[None]


def solution(mesh):
    placed = (P("state", "mode", None, None), P(), P(), P())
    return jax.shard_map(
        shards,
        mesh=mesh,
        in_specs=placed,
        out_specs=P("state", "mode", None, None),
        check_vma=False,
    )
```

time: 184 us -> 159 us (0.86)
  blocking collectives: 34.7 us -> 124 us
  waiting for transfers between devices: 66.7 us -> 0 us
  Pallas kernels: 0 us -> 35 us
  local copies, waits for them, and re-layouts: 31.7 us -> 0 us
  matrix products: 24.6 us -> 0 us
  starting transfers between devices: 21.9 us -> 0 us
  other arithmetic: 3.13 us -> 0 us
    all_to_all x1 -> x2, blocking collectives: 34.7 us -> 124 us  [the longest x1 86.8 us: shards(): got = lax.all_to_all(sent, EVERY, split_axis=0, concat_axis=0, tiled=True)]
    all_to_all x3 -> x0, waiting for transfers between devices: 66.7 us -> none  [shards(): lax.all_to_all(value, EVERY, split_axis=0, concat_axis=0, tiled=True)]
    pallas_call x0 -> x3, Pallas kernels: none -> 35 us  [the longest x1 19.1 us: shards(): pl.pallas_call(prepare, grid_spec=pltpu.PrefetchScalarGridSpec(num_scalar...]
    dot_general x9 -> x0, matrix products: 24.6 us -> none  [the longest x3 14.5 us: shards(): jnp.einsum('ab,bik->aik', own_second[term], inner, preferred_element_type...]
    all_to_all x3 -> x0, starting transfers between devices: 21.9 us -> none  [shards(): lax.all_to_all(value, EVERY, split_axis=0, concat_axis=0, tiled=True)]
    convert_element_type x5 -> x0, local copies, waits for them, and re-layouts: 16.8 us -> none  [the longest x3 12.3 us: shards(): prepared.append(jnp.einsum('ab,bik->aik', own_second[term], inner, prefer...]
    slice x3 -> x0, local copies, waits for them, and re-layouts: 8.97 us -> none  [shards(): pieces[term][source]]
    broadcast_in_dim x1 -> x0, local copies, waits for them, and re-layouts: 3.3 us -> none  [shards(): return relaxed[None]]
  transfers between devices with their start and end apart: 3 -> 0, of which waited for: 3 -> 0; matrix products, arithmetic and copies ran while one was open for 13% -> 0% of each run, Pallas kernels for 0% -> 0%
where the time goes in v2:
time: 159 us
  blocking collectives  124 us (78%)
  Pallas kernels  35 us (22%)
    all_to_all x1, blocking collectives, shards(): got = lax.all_to_all(sent, EVERY, split_axis=0, concat_axis=0, tiled=True)  86.8 us
    all_to_all x1, blocking collectives, shards(): lax.all_to_all(applied, EVERY, split_axis=0, concat_axis=0, tiled=True)  36.8 us
    pallas_call x1, Pallas kernels, shards(): pl.pallas_call(prepare, grid_spec=pltpu.PrefetchScalarGridSpec(num_scalar...  19.1 us
    pallas_call x1, Pallas kernels, shards(): pl.pallas_call(apply_first, in_specs=[whole, whole], out_specs=whole, out...  8.49 us
    pallas_call x1, Pallas kernels, shards(): pl.pallas_call(relax, grid=(rows,), in_specs=[pl.BlockSpec((devices, held...  7.47 us

profile of v2, /device:TPU:1, one launch (start us, length us, event | category | flops | bytes accessed | tf_op | source)
XLA Modules:
  0.0 158.6 jit_solution(8999168585391606689)
XLA Ops:
  0.0 19.1 %prepare.1 = bf16[128,3,32,256]{3,2,1,0:T(8,128)(2,1)} custom-call(s32[1]{0:T(128)} %bitcast.state_ref, bf16[8,512,256]{2,1,0:T(8,128)(2,1)} %bitcast.3, bf16[2,3,512,512]{3,2,1,0:T(8,128)(2,1)} %second_ref.1, bf16[2,3,256,256]{3,2,1,0:T(8,128)(2,1)} %third_ref.1), custom_call_target="tpu_custom_call" | custom-call | tf_op jit(solution)/shard_map/prepare/pallas_call | solution.py:94
  19.1 86.8 %all_to_all.10.got_ref = bf16[128,3,32,256]{3,2,1,0:T(8,128)(2,1)} all-to-all(bf16[128,3,32,256]{3,2,1,0:T(8,128)(2,1)} %prepare.1), channel_id=1, replica_groups=mesh['state'=2,'mode'=64] {'state','mode'}, dimensions={0} | all-to-all | bytes 12582912 | tf_op jit(solution)/shard_map/all_to_all | solution.py:116
  105.8 8.5 %apply_first.1 = bf16[128,32,256]{2,1,0:T(8,128)(2,1)} custom-call(bf16[2,3,512,512]{3,2,1,0:T(8,128)(2,1)} %first_ref.1, bf16[128,3,32,256]{3,2,1,0:T(8,128)(2,1)} %all_to_all.10.got_ref), custom_call_target="tpu_custom_call" | custom-call | tf_op jit(solution)/shard_map/apply_first/pallas_call | solution.py:117
  114.3 36.8 %all_to_all.11.got_ref = bf16[128,32,256]{2,1,0:T(8,128)(2,1)} all-to-all(bf16[128,32,256]{2,1,0:T(8,128)(2,1)} %apply_first.1), channel_id=1, replica_groups=mesh['state'=2,'mode'=64] {'state','mode'}, dimensions={0} | all-to-all | bytes 4194304 | tf_op jit(solution)/shard_map/all_to_all | solution.py:124
  151.1 7.5 %relax.1 = f32[8,512,256]{2,1,0:T(8,128)} custom-call(bf16[128,32,256]{2,1,0:T(8,128)(2,1)} %all_to_all.11.got_ref, bf16[8,512,256]{2,1,0:T(8,128)(2,1)} %bitcast.4), custom_call_target="tpu_custom_call" | custom-call | tf_op jit(solution)/shard_map/relax/pallas_call | solution.py:125

commit v3 on v2

--- a/solution.py
+++ b/solution.py
@@ -7,12 +7,14 @@
 
 EVERY = ("state", "mode")
 LANES = 128
+UNROLL = 8
 
 
 def prepare(state_ref, core_ref, second_ref, third_ref, sent_ref, rows_ref):
     rows, second_extent, third_extent = core_ref.shape
     second = second_ref[0, 0]
     third = third_ref[0, 0]
+    term = pl.program_id(0)
 
     def one_row(row, carry):
         inner = lax.dot_general(
@@ -28,9 +30,9 @@
             ]
         return carry
 
-    lax.fori_loop(0, rows, one_row, 0)
+    lax.fori_loop(0, rows, one_row, 0, unroll=UNROLL)
     for part in range(third_extent // LANES):
-        sent_ref[:, 0, :, part * LANES : (part + 1) * LANES] = (
+        sent_ref[:, term, :, part * LANES : (part + 1) * LANES] = (
             rows_ref[part].astype(jnp.bfloat16).reshape(*sent_ref.shape[:1], sent_ref.shape[2], LANES)
         )
 
@@ -79,7 +81,15 @@
     for part in range(rows_ref.shape[0]):
         lanes = slice(part * LANES, (part + 1) * LANES)
         applied = rows_ref[part, pl.ds(row, core_ref.shape[1], stride=rows), :]
-        relaxed_ref[0, :, lanes] = core_ref[0, :, lanes].astype(jnp.float32) - 0.5 * applied
+        relaxed_ref[0, :, lanes] = core_ref[row, :, lanes].astype(jnp.float32) - 0.5 * applied
+
+
+def in_vmem(value):
+    return pltpu.with_memory_space_constraint(value, pltpu.VMEM)
+
+
+def in_hbm(value):
+    return pltpu.with_memory_space_constraint(value, pltpu.HBM)
 
 
 def shards(core, op_one, op_two, op_three):
@@ -105,35 +115,33 @@
                     (1, 1, third_extent, third_extent), lambda term, state: (state[0], term, 0, 0)
                 ),
             ],
-            out_specs=pl.BlockSpec(
-                (devices, 1, held, third_extent), lambda term, state: (0, term, 0, 0)
-            ),
+            out_specs=whole,
             scratch_shapes=[pltpu.VMEM((third_extent // LANES, rows * second_extent, LANES), jnp.float32)],
         ),
-        out_shape=jax.ShapeDtypeStruct((devices, terms, held, third_extent), jnp.bfloat16),
+        out_shape=pltpu.VMEM((devices, terms, held, third_extent), jnp.bfloat16),
+        compiler_params=pltpu.CompilerParams(vmem_limit_bytes=32 << 20),
         name="prepare",
-    )(state_index, own_core, op_two, op_three)
+    )(state_index, in_hbm(own_core), in_hbm(op_two), in_hbm(op_three))
     got = lax.all_to_all(sent, EVERY, split_axis=0, concat_axis=0, tiled=True)
     applied = pl.pallas_call(
         apply_first,
         in_specs=[whole, whole],
         out_specs=whole,
-        out_shape=jax.ShapeDtypeStruct((devices, held, third_extent), jnp.bfloat16),
+        out_shape=pltpu.VMEM((devices, held, third_extent), jnp.bfloat16),
+        compiler_params=pltpu.CompilerParams(vmem_limit_bytes=16 << 20),
         name="apply_first",
-    )(op_one, got)
+    )(in_vmem(op_one), in_vmem(got))
     returned = lax.all_to_all(applied, EVERY, split_axis=0, concat_axis=0, tiled=True)
     relaxed = pl.pallas_call(
         relax,
         grid=(rows,),
-        in_specs=[
-            pl.BlockSpec((devices, held, third_extent), lambda row: (0, 0, 0)),
-            pl.BlockSpec((1, second_extent, third_extent), lambda row: (row, 0, 0)),
-        ],
+        in_specs=[whole, whole],
         out_specs=pl.BlockSpec((1, second_extent, third_extent), lambda row: (row, 0, 0)),
         scratch_shapes=[pltpu.VMEM((third_extent // LANES, rows * second_extent, LANES), jnp.float32)],
         out_shape=jax.ShapeDtypeStruct(own_core.shape, jnp.float32),
+        compiler_params=pltpu.CompilerParams(vmem_limit_bytes=24 << 20),
         name="relax",
-    )(returned, own_core)
+    )(in_vmem(returned), in_vmem(own_core))
     return relaxed[None]
 
 

time: 159 us -> 140 us (0.88)
  Pallas kernels: 35 us -> 17.2 us
    pallas_call x1, Pallas kernels: 19.1 us -> 9.54 us  [shards(): pl.pallas_call(prepare, grid_spec=pltpu.PrefetchScalarGridSpec(num_scalar...]
    pallas_call x1, Pallas kernels: 8.49 us -> 3.43 us  [shards(): pl.pallas_call(apply_first, in_specs=[whole, whole], out_specs=whole, out...]
    pallas_call x1, Pallas kernels: 7.47 us -> 4.24 us  [shards(): pl.pallas_call(relax, grid=(rows,), in_specs=[whole, whole], out_specs=pl...]
where the time goes in v3:
time: 140 us
  blocking collectives  123 us (88%)
  Pallas kernels  17.2 us (12%)
    all_to_all x1, blocking collectives, shards(): got = lax.all_to_all(sent, EVERY, split_axis=0, concat_axis=0, tiled=True)  86.4 us
    all_to_all x1, blocking collectives, shards(): lax.all_to_all(applied, EVERY, split_axis=0, concat_axis=0, tiled=True)  36.5 us
    pallas_call x1, Pallas kernels, shards(): pl.pallas_call(prepare, grid_spec=pltpu.PrefetchScalarGridSpec(num_scalar...  9.54 us
    pallas_call x1, Pallas kernels, shards(): pl.pallas_call(relax, grid=(rows,), in_specs=[whole, whole], out_specs=pl...  4.24 us
    pallas_call x1, Pallas kernels, shards(): pl.pallas_call(apply_first, in_specs=[whole, whole], out_specs=whole, out...  3.43 us

profile of v3, /device:TPU:1, one launch (start us, length us, event | category | flops | bytes accessed | tf_op | source)
XLA Modules:
  0.0 140.2 jit_solution(833107157061821695)
XLA Ops:
  0.0 9.5 %prepare.1 = bf16[128,3,32,256]{3,2,1,0:T(8,128)(2,1)S(1)} custom-call(s32[1]{0:T(128)} %bitcast.state_ref, bf16[8,512,256]{2,1,0:T(8,128)(2,1)} %bitcast.3, bf16[2,3,512,512]{3,2,1,0:T(8,128)(2,1)} %second_ref.1, bf16[2,3,256,256]{3,2,1,0:T(8,128)(2,1)} %third_ref.1), custom_call_target="tpu_custom_call" | custom-call | tf_op jit(solution)/shard_map/prepare/pallas_call | solution.py:104
  9.5 0.0 copy-start.1
  9.6 86.4 %all_to_all.10.got_ref = bf16[128,3,32,256]{3,2,1,0:T(8,128)(2,1)S(1)} all-to-all(bf16[128,3,32,256]{3,2,1,0:T(8,128)(2,1)S(1)} %prepare.1), channel_id=1, replica_groups=mesh['state'=2,'mode'=64] {'state','mode'}, dimensions={0} | all-to-all | bytes 12582912 | tf_op jit(solution)/shard_map/all_to_all | solution.py:125
  96.0 0.0 copy-done.1
  96.0 3.4 %apply_first.1 = bf16[128,32,256]{2,1,0:T(8,128)(2,1)S(1)} custom-call(bf16[2,3,512,512]{3,2,1,0:T(8,128)(2,1)S(1)} %copy-done.1, bf16[128,3,32,256]{3,2,1,0:T(8,128)(2,1)S(1)} %all_to_all.10.got_ref), custom_call_target="tpu_custom_call" | custom-call | tf_op jit(solution)/shard_map/apply_first/pallas_call | solution.py:126
  99.4 0.0 copy-start
  99.5 36.5 %all_to_all.11.got_ref = bf16[128,32,256]{2,1,0:T(8,128)(2,1)S(1)} all-to-all(bf16[128,32,256]{2,1,0:T(8,128)(2,1)S(1)} %apply_first.1), channel_id=1, replica_groups=mesh['state'=2,'mode'=64] {'state','mode'}, dimensions={0} | all-to-all | bytes 4194304 | tf_op jit(solution)/shard_map/all_to_all | solution.py:134
  135.9 0.0 copy-done
  135.9 4.2 %relax.1 = f32[8,512,256]{2,1,0:T(8,128)} custom-call(bf16[128,32,256]{2,1,0:T(8,128)(2,1)S(1)} %all_to_all.11.got_ref, bf16[8,512,256]{2,1,0:T(8,128)(2,1)S(1)} %bitcast.4), custom_call_target="tpu_custom_call" | custom-call | tf_op jit(solution)/shard_map/relax/pallas_call | solution.py:135
Async XLA Ops:
  9.5 86.5 %copy-start.1 = (bf16[2,3,512,512]{3,2,1,0:T(8,128)(2,1)S(1)}, bf16[2,3,512,512]{3,2,1,0:T(8,128)(2,1)}, u32[]{:S(2)}) copy-start(bf16[2,3,512,512]{3,2,1,0:T(8,128)(2,1)} %first_ref.1) | copy-start | bytes 9437188
  99.4 36.5 %copy-start = (bf16[1,8,512,256]{3,2,1,0:T(8,128)(2,1)S(1)}, bf16[1,8,512,256]{3,2,1,0:T(8,128)(2,1)}, u32[]{:S(2)}) copy-start(bf16[1,8,512,256]{3,2,1,0:T(8,128)(2,1)} %param.4) | copy-start | bytes 6291460

commit v4 on v3

v4 whole, which is shorter than its diff:
```python
import jax
import jax.numpy as jnp
from jax import lax
from jax.experimental import pallas as pl
from jax.experimental.pallas import tpu as pltpu
from jax.sharding import PartitionSpec as P

EVERY = ("state", "mode")
LANES = 128
PITCH = 12
GROUP = 4
BLOCKS = 8


def prepare(state_ref, core_ref, second_ref, third_ref, sent_ref, inner_ref, rows_ref):
    rows, second_extent, third_extent = core_ref.shape
    devices, _, parts, held, _ = sent_ref.shape
    second = second_ref[0, 0]
    third = third_ref[0, 0]
    term = pl.program_id(0)
    for row in range(rows):
        inner_ref[:, row * third_extent : (row + 1) * third_extent] = lax.dot_general(
            core_ref[row],
            third,
            (((1,), (1,)), ((), ())),
            preferred_element_type=jnp.float32,
        ).astype(jnp.bfloat16)
    for first in range(0, rows, GROUP):
        value = jnp.dot(
            second,
            inner_ref[:, first * third_extent : (first + GROUP) * third_extent],
            preferred_element_type=jnp.float32,
        )
        for row in range(GROUP):
            for part in range(parts):
                lane = row * third_extent + part * LANES
                rows_ref[part, pl.ds(first + row, second_extent, stride=PITCH), :] = value[
                    :, lane : lane + LANES
                ]
    for part in range(parts):
        turned = jnp.stack(
            [rows_ref[part, at * PITCH : at * PITCH + rows] for at in range(second_extent)]
        )
        sent_ref[:, term, part] = turned.astype(jnp.bfloat16).reshape(devices, held, LANES)


def apply_first(first_ref, got_ref, sent_ref):
    states, _, first_extent, _ = first_ref.shape
    devices, _, parts, held, _ = got_ref.shape
    owners = devices // states
    rows = first_extent // owners

    def piece(source, term, column):
        values = [
            got_ref[
                source * owners : (source + 1) * owners,
                term,
                part,
                column * rows : (column + 1) * rows,
            ]
            .astype(jnp.float32)
            .reshape(first_extent, LANES)
            .astype(jnp.bfloat16)
            for part in range(parts)
        ]
        return jnp.concatenate(values, axis=1)

    for column in range(held // rows):
        for state in range(states):
            total = jnp.zeros((first_extent, parts * LANES), jnp.float32)
            for source, term in ((state, 0), (state, 1), (1 - state, 2)):
                total += jnp.dot(
                    first_ref[source, term],
                    piece(source, term, column),
                    preferred_element_type=jnp.float32,
                )
            for part in range(parts):
                sent_ref[
                    state * owners : (state + 1) * owners,
                    part,
                    column * rows : (column + 1) * rows,
                ] = (
                    total[:, part * LANES : (part + 1) * LANES]
                    .reshape(owners, rows, LANES)
                    .astype(jnp.bfloat16)
                )


def relax(got_ref, core_ref, relaxed_ref, rows_ref):
    block = pl.program_id(0)
    rows, columns, _ = relaxed_ref.shape
    _, parts, held, _ = got_ref.shape
    owners = columns * rows // held
    for part in range(parts):
        value = got_ref[pl.ds(block * owners, owners), part].astype(jnp.float32)
        value = value.reshape(columns, rows, LANES)
        for column in range(columns):
            rows_ref[part, column * PITCH : column * PITCH + rows] = value[column]
    for row in range(rows):
        for part in range(parts):
            lanes = slice(part * LANES, (part + 1) * LANES)
            applied = rows_ref[part, pl.ds(row, columns, stride=PITCH), :]
            kept = core_ref[row, pl.ds(block * columns, columns), lanes]
            relaxed_ref[row, :, lanes] = kept.astype(jnp.float32) - 0.5 * applied


def in_vmem(value):
    return pltpu.with_memory_space_constraint(value, pltpu.VMEM)


def in_hbm(value):
    return pltpu.with_memory_space_constraint(value, pltpu.HBM)


def shards(core, op_one, op_two, op_three):
    own_core = core[0]
    rows, second_extent, third_extent = own_core.shape
    states, terms, first_extent, _ = op_one.shape
    devices = states * (first_extent // rows)
    held = second_extent // devices * rows
    parts = third_extent // LANES
    columns = second_extent // BLOCKS
    state_index = lax.axis_index("state").astype(jnp.int32).reshape(1)
    whole = pl.BlockSpec(memory_space=pltpu.VMEM)

    sent = pl.pallas_call(
        prepare,
        grid_spec=pltpu.PrefetchScalarGridSpec(
            num_scalar_prefetch=1,
            grid=(terms,),
            in_specs=[
                pl.BlockSpec((rows, second_extent, third_extent), lambda term, state: (0, 0, 0)),
                pl.BlockSpec(
                    (1, 1, second_extent, second_extent), lambda term, state: (state[0], term, 0, 0)
                ),
                pl.BlockSpec(
                    (1, 1, third_extent, third_extent), lambda term, state: (state[0], term, 0, 0)
                ),
            ],
            out_specs=whole,
            scratch_shapes=[
                pltpu.VMEM((second_extent, rows * third_extent), jnp.bfloat16),
                pltpu.VMEM((parts, second_extent * PITCH, LANES), jnp.float32),
            ],
        ),
        out_shape=pltpu.VMEM((devices, terms, parts, held, LANES), jnp.bfloat16),
        compiler_params=pltpu.CompilerParams(vmem_limit_bytes=36 << 20),
        name="prepare",
    )(state_index, in_hbm(own_core), in_hbm(op_two), in_hbm(op_three))
    got = lax.all_to_all(sent, EVERY, split_axis=0, concat_axis=0, tiled=True)
    applied = pl.pallas_call(
        apply_first,
        in_specs=[whole, whole],
        out_specs=whole,
        out_shape=pltpu.VMEM((devices, parts, held, LANES), jnp.bfloat16),
        compiler_params=pltpu.CompilerParams(vmem_limit_bytes=16 << 20),
        name="apply_first",
    )(in_vmem(op_one), in_vmem(got))
    returned = lax.all_to_all(applied, EVERY, split_axis=0, concat_axis=0, tiled=True)
    relaxed = pl.pallas_call(
        relax,
        grid=(BLOCKS,),
        in_specs=[whole, whole],
        out_specs=pl.BlockSpec((rows, columns, third_extent), lambda block: (0, block, 0)),
        scratch_shapes=[pltpu.VMEM((parts, columns * PITCH, LANES), jnp.float32)],
        out_shape=jax.ShapeDtypeStruct(own_core.shape, jnp.float32),
        compiler_params=pltpu.CompilerParams(vmem_limit_bytes=24 << 20),
        name="relax",
    )(in_vmem(returned), in_vmem(own_core))
    return relaxed[None]


def solution(mesh):
    placed = (P("state", "mode", None, None), P(), P(), P())
    return jax.shard_map(
        shards,
        mesh=mesh,
        in_specs=placed,
        out_specs=P("state", "mode", None, None),
        check_vma=False,
    )
```

time: 140 us -> 138 us (0.986)
  Pallas kernels: 17.2 us -> 14.9 us
    pallas_call x1, Pallas kernels: 9.54 us -> 7.72 us  [shards(): pl.pallas_call(prepare, grid_spec=pltpu.PrefetchScalarGridSpec(num_scalar...]
where the time goes in v4:
time: 138 us
  blocking collectives  123 us (89%)
  Pallas kernels  14.9 us (11%)
    all_to_all x1, blocking collectives, shards(): got = lax.all_to_all(sent, EVERY, split_axis=0, concat_axis=0, tiled=True)  86.4 us
    all_to_all x1, blocking collectives, shards(): lax.all_to_all(applied, EVERY, split_axis=0, concat_axis=0, tiled=True)  36.5 us
    pallas_call x1, Pallas kernels, shards(): pl.pallas_call(prepare, grid_spec=pltpu.PrefetchScalarGridSpec(num_scalar...  7.72 us
    pallas_call x1, Pallas kernels, shards(): pl.pallas_call(relax, grid=(BLOCKS,), in_specs=[whole, whole], out_specs=...  3.7 us
    pallas_call x1, Pallas kernels, shards(): pl.pallas_call(apply_first, in_specs=[whole, whole], out_specs=whole, out...  3.43 us

profile of v4, /device:TPU:1, one launch (start us, length us, event | category | flops | bytes accessed | tf_op | source)
XLA Modules:
  0.0 137.8 jit_solution(12169557138559467457)
XLA Ops:
  0.0 7.7 %prepare.1 = bf16[128,3,2,32,128]{4,3,2,1,0:T(8,128)(2,1)S(1)} custom-call(s32[1]{0:T(128)} %bitcast.state_ref, bf16[8,512,256]{2,1,0:T(8,128)(2,1)} %bitcast.3, bf16[2,3,512,512]{3,2,1,0:T(8,128)(2,1)} %second_ref.1, bf16[2,3,256,256]{3,2,1,0:T(8,128)(2,1)} %third_ref.1), custom_call_target="tpu_custom_call" | custom-call | tf_op jit(solution)/shard_map/prepare/pallas_call | solution.py:126
  7.7 0.0 copy-start.1
  7.7 86.4 %all_to_all.10.got_ref = bf16[128,3,2,32,128]{4,3,2,1,0:T(8,128)(2,1)S(1)} all-to-all(bf16[128,3,2,32,128]{4,3,2,1,0:T(8,128)(2,1)S(1)} %prepare.1), channel_id=1, replica_groups=mesh['state'=2,'mode'=64] {'state','mode'}, dimensions={0} | all-to-all | bytes 12582912 | tf_op jit(solution)/shard_map/all_to_all | solution.py:150
  94.2 0.0 copy-done.1
  94.2 3.4 %apply_first.1 = bf16[128,2,32,128]{3,2,1,0:T(8,128)(2,1)S(1)} custom-call(bf16[2,3,512,512]{3,2,1,0:T(8,128)(2,1)S(1)} %copy-done.1, bf16[128,3,2,32,128]{4,3,2,1,0:T(8,128)(2,1)S(1)} %all_to_all.10.got_ref), custom_call_target="tpu_custom_call" | custom-call | tf_op jit(solution)/shard_map/apply_first/pallas_call | solution.py:151
  97.6 0.0 copy-start
  97.6 36.5 %all_to_all.11.got_ref = bf16[128,2,32,128]{3,2,1,0:T(8,128)(2,1)S(1)} all-to-all(bf16[128,2,32,128]{3,2,1,0:T(8,128)(2,1)S(1)} %apply_first.1), channel_id=1, replica_groups=mesh['state'=2,'mode'=64] {'state','mode'}, dimensions={0} | all-to-all | bytes 4194304 | tf_op jit(solution)/shard_map/all_to_all | solution.py:159
  134.1 0.0 copy-done
  134.1 3.7 %relax.1 = f32[8,512,256]{2,1,0:T(8,128)} custom-call(bf16[128,2,32,128]{3,2,1,0:T(8,128)(2,1)S(1)} %all_to_all.11.got_ref, bf16[8,512,256]{2,1,0:T(8,128)(2,1)S(1)} %bitcast.4), custom_call_target="tpu_custom_call" | custom-call | tf_op jit(solution)/shard_map/relax/pallas_call | solution.py:160
Async XLA Ops:
  7.7 86.5 %copy-start.1 = (bf16[2,3,512,512]{3,2,1,0:T(8,128)(2,1)S(1)}, bf16[2,3,512,512]{3,2,1,0:T(8,128)(2,1)}, u32[]{:S(2)}) copy-start(bf16[2,3,512,512]{3,2,1,0:T(8,128)(2,1)} %first_ref.1) | copy-start | bytes 9437188
  97.6 36.5 %copy-start = (bf16[1,8,512,256]{3,2,1,0:T(8,128)(2,1)S(1)}, bf16[1,8,512,256]{3,2,1,0:T(8,128)(2,1)}, u32[]{:S(2)}) copy-start(bf16[1,8,512,256]{3,2,1,0:T(8,128)(2,1)} %param.4) | copy-start | bytes 6291460

commit v5 on v4

--- a/solution.py
+++ b/solution.py
@@ -8,8 +8,9 @@
 EVERY = ("state", "mode")
 LANES = 128
 PITCH = 12
-GROUP = 4
-BLOCKS = 8
+GROUP = 2
+BLOCKS = 2
+SIDE = 4
 
 
 def prepare(state_ref, core_ref, second_ref, third_ref, sent_ref, inner_ref, rows_ref):
@@ -18,19 +19,25 @@
     second = second_ref[0, 0]
     third = third_ref[0, 0]
     term = pl.program_id(0)
-    for row in range(rows):
-        inner_ref[:, row * third_extent : (row + 1) * third_extent] = lax.dot_general(
+    def stage(row):
+        inner = lax.dot_general(
             core_ref[row],
             third,
             (((1,), (1,)), ((), ())),
             preferred_element_type=jnp.float32,
         ).astype(jnp.bfloat16)
+        for part in range(parts):
+            inner_ref[row, part] = inner[:, part * LANES : (part + 1) * LANES]
+
+    for row in range(GROUP):
+        stage(row)
     for first in range(0, rows, GROUP):
-        value = jnp.dot(
-            second,
-            inner_ref[:, first * third_extent : (first + GROUP) * third_extent],
-            preferred_element_type=jnp.float32,
+        for row in range(first + GROUP, min(first + 2 * GROUP, rows)):
+            stage(row)
+        inner = jnp.concatenate(
+            [inner_ref[first + row, part] for row in range(GROUP) for part in range(parts)], axis=1
         )
+        value = jnp.dot(second, inner, preferred_element_type=jnp.float32)
         for row in range(GROUP):
             for part in range(parts):
                 lane = row * third_extent + part * LANES
@@ -65,25 +72,28 @@
         ]
         return jnp.concatenate(values, axis=1)
 
-    for column in range(held // rows):
+    for first in range(0, held // rows, SIDE):
+        columns = range(first, first + SIDE)
         for state in range(states):
-            total = jnp.zeros((first_extent, parts * LANES), jnp.float32)
+            total = jnp.zeros((first_extent, SIDE * parts * LANES), jnp.float32)
             for source, term in ((state, 0), (state, 1), (1 - state, 2)):
                 total += jnp.dot(
                     first_ref[source, term],
-                    piece(source, term, column),
+                    jnp.concatenate([piece(source, term, column) for column in columns], axis=1),
                     preferred_element_type=jnp.float32,
                 )
-            for part in range(parts):
-                sent_ref[
-                    state * owners : (state + 1) * owners,
-                    part,
-                    column * rows : (column + 1) * rows,
-                ] = (
-                    total[:, part * LANES : (part + 1) * LANES]
-                    .reshape(owners, rows, LANES)
-                    .astype(jnp.bfloat16)
-                )
+            for column in columns:
+                for part in range(parts):
+                    lane = ((column - first) * parts + part) * LANES
+                    sent_ref[
+                        state * owners : (state + 1) * owners,
+                        part,
+                        column * rows : (column + 1) * rows,
+                    ] = (
+                        total[:, lane : lane + LANES]
+                        .reshape(owners, rows, LANES)
+                        .astype(jnp.bfloat16)
+                    )
 
 
 def relax(got_ref, core_ref, relaxed_ref, rows_ref):
@@ -139,7 +149,7 @@
             ],
             out_specs=whole,
             scratch_shapes=[
-                pltpu.VMEM((second_extent, rows * third_extent), jnp.bfloat16),
+                pltpu.VMEM((rows, parts, second_extent, LANES), jnp.bfloat16),
                 pltpu.VMEM((parts, second_extent * PITCH, LANES), jnp.float32),
             ],
         ),

time: 138 us -> 137 us (level)
  no operation moved by 1% of the time
where the time goes in v5:
time: 137 us
  blocking collectives  123 us (90%)
  Pallas kernels  13.8 us (10%)
    all_to_all x1, blocking collectives, shards(): got = lax.all_to_all(sent, EVERY, split_axis=0, concat_axis=0, tiled=True)  86.4 us
    all_to_all x1, blocking collectives, shards(): lax.all_to_all(applied, EVERY, split_axis=0, concat_axis=0, tiled=True)  36.5 us
    pallas_call x1, Pallas kernels, shards(): pl.pallas_call(prepare, grid_spec=pltpu.PrefetchScalarGridSpec(num_scalar...  7.83 us
    pallas_call x1, Pallas kernels, shards(): pl.pallas_call(apply_first, in_specs=[whole, whole], out_specs=whole, out...  3.41 us

profile of v5, /device:TPU:1, one launch (start us, length us, event | category | flops | bytes accessed | tf_op | source)
XLA Modules:
  0.0 136.7 jit_solution(12157936842972934342)
XLA Ops:
  0.0 7.8 %prepare.1 = bf16[128,3,2,32,128]{4,3,2,1,0:T(8,128)(2,1)S(1)} custom-call(s32[1]{0:T(128)} %bitcast.state_ref, bf16[8,512,256]{2,1,0:T(8,128)(2,1)} %bitcast.3, bf16[2,3,512,512]{3,2,1,0:T(8,128)(2,1)} %second_ref.1, bf16[2,3,256,256]{3,2,1,0:T(8,128)(2,1)} %third_ref.1), custom_call_target="tpu_custom_call" | custom-call | tf_op jit(solution)/shard_map/prepare/pallas_call | solution.py:136
  7.8 0.0 copy-start.1
  7.9 86.4 %all_to_all.10.got_ref = bf16[128,3,2,32,128]{4,3,2,1,0:T(8,128)(2,1)S(1)} all-to-all(bf16[128,3,2,32,128]{4,3,2,1,0:T(8,128)(2,1)S(1)} %prepare.1), channel_id=1, replica_groups=mesh['state'=2,'mode'=64] {'state','mode'}, dimensions={0} | all-to-all | bytes 12582912 | tf_op jit(solution)/shard_map/all_to_all | solution.py:160
  94.3 0.0 copy-done.1
  94.3 3.4 %apply_first.1 = bf16[128,2,32,128]{3,2,1,0:T(8,128)(2,1)S(1)} custom-call(bf16[2,3,512,512]{3,2,1,0:T(8,128)(2,1)S(1)} %copy-done.1, bf16[128,3,2,32,128]{4,3,2,1,0:T(8,128)(2,1)S(1)} %all_to_all.10.got_ref), custom_call_target="tpu_custom_call" | custom-call | tf_op jit(solution)/shard_map/apply_first/pallas_call | solution.py:161
  97.7 0.0 copy-start
  97.7 36.5 %all_to_all.11.got_ref = bf16[128,2,32,128]{3,2,1,0:T(8,128)(2,1)S(1)} all-to-all(bf16[128,2,32,128]{3,2,1,0:T(8,128)(2,1)S(1)} %apply_first.1), channel_id=1, replica_groups=mesh['state'=2,'mode'=64] {'state','mode'}, dimensions={0} | all-to-all | bytes 4194304 | tf_op jit(solution)/shard_map/all_to_all | solution.py:169
  134.2 0.0 copy-done
  134.2 2.5 %relax.1 = f32[8,512,256]{2,1,0:T(8,128)} custom-call(bf16[128,2,32,128]{3,2,1,0:T(8,128)(2,1)S(1)} %all_to_all.11.got_ref, bf16[8,512,256]{2,1,0:T(8,128)(2,1)S(1)} %bitcast.4), custom_call_target="tpu_custom_call" | custom-call | tf_op jit(solution)/shard_map/relax/pallas_call | solution.py:170
Async XLA Ops:
  7.8 86.4 %copy-start.1 = (bf16[2,3,512,512]{3,2,1,0:T(8,128)(2,1)S(1)}, bf16[2,3,512,512]{3,2,1,0:T(8,128)(2,1)}, u32[]{:S(2)}) copy-start(bf16[2,3,512,512]{3,2,1,0:T(8,128)(2,1)} %first_ref.1) | copy-start | bytes 9437188
  97.7 36.5 %copy-start = (bf16[1,8,512,256]{3,2,1,0:T(8,128)(2,1)S(1)}, bf16[1,8,512,256]{3,2,1,0:T(8,128)(2,1)}, u32[]{:S(2)}) copy-start(bf16[1,8,512,256]{3,2,1,0:T(8,128)(2,1)} %param.4) | copy-start | bytes 6291460

commit v6 on v5

v6 whole, which is shorter than its diff:
```python
import jax
import jax.numpy as jnp
from jax import lax
from jax.experimental import pallas as pl
from jax.experimental.pallas import tpu as pltpu
from jax.sharding import PartitionSpec as P

EVERY = ("state", "mode")
LANES = 128
HALF = 4
PITCH = 12
GROUP = 2
BLOCKS = 4
SIDE = 4


def prepare(
    state_ref,
    core_hbm,
    second_hbm,
    third_hbm,
    sent_ref,
    core_ref,
    second_ref,
    third_ref,
    inner_ref,
    rows_ref,
    core_sems,
    second_sems,
    third_sems,
):
    rows, second_extent, third_extent = core_ref.shape
    devices, terms, parts, held, _ = sent_ref.shape
    state = state_ref[0]
    groups = range(0, rows, GROUP)
    cores = {
        first: pltpu.make_async_copy(
            core_hbm.at[pl.ds(first, HALF)],
            core_ref.at[pl.ds(first, HALF)],
            core_sems.at[first // HALF],
        )
        for first in range(0, rows, HALF)
    }
    seconds = [
        pltpu.make_async_copy(second_hbm.at[state, term], second_ref.at[term], second_sems.at[term])
        for term in range(terms)
    ]
    thirds = [
        pltpu.make_async_copy(third_hbm.at[state, term], third_ref.at[term], third_sems.at[term])
        for term in range(terms)
    ]

    def stage(term, first):
        for row in range(first, first + GROUP):
            inner = lax.dot_general(
                core_ref[row],
                third_ref[term],
                (((1,), (1,)), ((), ())),
                preferred_element_type=jnp.float32,
            ).astype(jnp.bfloat16)
            for part in range(parts):
                inner_ref[row, part] = inner[:, part * LANES : (part + 1) * LANES]

    def spread(term, first):
        inner = jnp.concatenate(
            [inner_ref[first + row, part] for row in range(GROUP) for part in range(parts)], axis=1
        )
        value = jnp.dot(second_ref[term], inner, preferred_element_type=jnp.float32)
        for row in range(GROUP):
            for part in range(parts):
                lane = row * third_extent + part * LANES
                rows_ref[term % 2, part, pl.ds(first + row, second_extent, stride=PITCH), :] = value[
                    :, lane : lane + LANES
                ]

    def send(term, first, count):
        owners = count * rows // held
        low = first * rows // held
        for part in range(parts):
            turned = jnp.stack(
                [
                    rows_ref[term % 2, part, at * PITCH : at * PITCH + rows]
                    for at in range(first, first + count)
                ]
            )
            sent_ref[low : low + owners, term, part] = turned.astype(jnp.bfloat16).reshape(
                owners, held, LANES
            )

    thirds[0].start()
    seconds[0].start()
    for first in range(0, rows, HALF):
        cores[first].start()
    for term in range(1, terms):
        thirds[term].start()
        seconds[term].start()
    thirds[0].wait()
    seconds[0].wait()
    for half in range(0, rows, HALF):
        cores[half].wait()
        stage(0, half)
        for first in range(half, half + HALF, GROUP):
            if first + GROUP < half + HALF:
                stage(0, first + GROUP)
            spread(0, first)
    for term in range(1, terms):
        thirds[term].wait()
        seconds[term].wait()
    share = second_extent // len(groups)
    for term in range(1, terms):
        stage(term, 0)
        for turn, first in enumerate(groups):
            if first + GROUP < rows:
                stage(term, first + GROUP)
            spread(term, first)
            send(term - 1, turn * share, share)
    send(terms - 1, 0, second_extent)


def apply_first(first_ref, got_ref, sent_ref):
    states, _, first_extent, _ = first_ref.shape
    devices, _, parts, held, _ = got_ref.shape
    owners = devices // states
    rows = first_extent // owners

    def piece(source, term, column):
        values = [
            got_ref[
                source * owners : (source + 1) * owners,
                term,
                part,
                column * rows : (column + 1) * rows,
            ]
            .astype(jnp.float32)
            .reshape(first_extent, LANES)
            .astype(jnp.bfloat16)
            for part in range(parts)
        ]
        return jnp.concatenate(values, axis=1)

    for first in range(0, held // rows, SIDE):
        columns = range(first, first + SIDE)
        for state in range(states):
            total = jnp.zeros((first_extent, SIDE * parts * LANES), jnp.float32)
            for source, term in ((state, 0), (state, 1), (1 - state, 2)):
                total += jnp.dot(
                    first_ref[source, term],
                    jnp.concatenate([piece(source, term, column) for column in columns], axis=1),
                    preferred_element_type=jnp.float32,
                )
            for column in columns:
                for part in range(parts):
                    lane = ((column - first) * parts + part) * LANES
                    sent_ref[
                        state * owners : (state + 1) * owners,
                        part,
                        column * rows : (column + 1) * rows,
                    ] = (
                        total[:, lane : lane + LANES]
                        .reshape(owners, rows, LANES)
                        .astype(jnp.bfloat16)
                    )


def relax(got_ref, core_ref, relaxed_hbm, rows_ref, out_ref, sems):
    rows, second_extent, _ = core_ref.shape
    _, parts, held, _ = got_ref.shape
    columns = second_extent // BLOCKS
    owners = columns * rows // held
    copies = []
    for block in range(BLOCKS):
        low = block * columns
        for part in range(parts):
            value = got_ref[block * owners : (block + 1) * owners, part].astype(jnp.float32)
            value = value.reshape(columns, rows, LANES)
            for column in range(columns):
                at = (low + column) * PITCH
                rows_ref[part, at : at + rows] = value[column]
        for row in range(rows):
            for part in range(parts):
                lanes = slice(part * LANES, (part + 1) * LANES)
                applied = rows_ref[part, pl.ds(low * PITCH + row, columns, stride=PITCH), :]
                kept = core_ref[row, low : low + columns, lanes]
                out_ref[row, low : low + columns, lanes] = (
                    kept.astype(jnp.float32) - 0.5 * applied
                )
        copies.append(
            pltpu.make_async_copy(
                out_ref.at[:, pl.ds(low, columns)],
                relaxed_hbm.at[:, pl.ds(low, columns)],
                sems.at[block],
            )
        )
        copies[-1].start()
    for copy in copies:
        copy.wait()


def in_vmem(value):
    return pltpu.with_memory_space_constraint(value, pltpu.VMEM)


def in_hbm(value):
    return pltpu.with_memory_space_constraint(value, pltpu.HBM)


def shards(core, op_one, op_two, op_three):
    own_core = core[0]
    rows, second_extent, third_extent = own_core.shape
    states, terms, first_extent, _ = op_one.shape
    devices = states * (first_extent // rows)
    held = second_extent // devices * rows
    parts = third_extent // LANES
    state_index = lax.axis_index("state").astype(jnp.int32).reshape(1)
    whole = pl.BlockSpec(memory_space=pltpu.VMEM)

    sent = pl.pallas_call(
        prepare,
        in_specs=[pl.BlockSpec(memory_space=pltpu.SMEM)]
        + [pl.BlockSpec(memory_space=pltpu.HBM)] * 3,
        out_specs=whole,
        scratch_shapes=[
            pltpu.VMEM((rows, second_extent, third_extent), jnp.bfloat16),
            pltpu.VMEM((terms, second_extent, second_extent), jnp.bfloat16),
            pltpu.VMEM((terms, third_extent, third_extent), jnp.bfloat16),
            pltpu.VMEM((rows, parts, second_extent, LANES), jnp.bfloat16),
            pltpu.VMEM((2, parts, second_extent * PITCH, LANES), jnp.float32),
            pltpu.SemaphoreType.DMA((rows // HALF,)),
            pltpu.SemaphoreType.DMA((terms,)),
            pltpu.SemaphoreType.DMA((terms,)),
        ],
        out_shape=pltpu.VMEM((devices, terms, parts, held, LANES), jnp.bfloat16),
        compiler_params=pltpu.CompilerParams(vmem_limit_bytes=36 << 20),
        name="prepare",
    )(state_index, in_hbm(own_core), in_hbm(op_two), in_hbm(op_three))
    got = lax.all_to_all(sent, EVERY, split_axis=0, concat_axis=0, tiled=True)
    applied = pl.pallas_call(
        apply_first,
        in_specs=[whole, whole],
        out_specs=whole,
        out_shape=pltpu.VMEM((devices, parts, held, LANES), jnp.bfloat16),
        compiler_params=pltpu.CompilerParams(vmem_limit_bytes=16 << 20),
        name="apply_first",
    )(in_vmem(op_one), in_vmem(got))
    returned = lax.all_to_all(applied, EVERY, split_axis=0, concat_axis=0, tiled=True)
    relaxed = pl.pallas_call(
        relax,
        in_specs=[whole, whole],
        out_specs=pl.BlockSpec(memory_space=pltpu.HBM),
        scratch_shapes=[
            pltpu.VMEM((parts, second_extent * PITCH, LANES), jnp.float32),
            pltpu.VMEM(own_core.shape, jnp.float32),
            pltpu.SemaphoreType.DMA((BLOCKS,)),
        ],
        out_shape=jax.ShapeDtypeStruct(own_core.shape, jnp.float32),
        compiler_params=pltpu.CompilerParams(vmem_limit_bytes=24 << 20),
        name="relax",
    )(in_vmem(returned), in_vmem(own_core))
    return relaxed[None]


def solution(mesh):
    placed = (P("state", "mode", None, None), P(), P(), P())
    return jax.shard_map(
        shards,
        mesh=mesh,
        in_specs=placed,
        out_specs=P("state", "mode", None, None),
        check_vma=False,
    )
```

time: 137 us -> 136 us (level)
  no operation moved by 1% of the time
where the time goes in v6:
time: 136 us
  blocking collectives  123 us (90%)
  Pallas kernels  13.1 us (10%)
    all_to_all x1, blocking collectives, shards(): got = lax.all_to_all(sent, EVERY, split_axis=0, concat_axis=0, tiled=True)  86.4 us
    all_to_all x1, blocking collectives, shards(): lax.all_to_all(applied, EVERY, split_axis=0, concat_axis=0, tiled=True)  36.5 us
    pallas_call x1, Pallas kernels, shards(): pl.pallas_call(prepare, in_specs=[pl.BlockSpec(memory_space=pltpu.SMEM)]...  7.47 us
    pallas_call x1, Pallas kernels, shards(): pl.pallas_call(apply_first, in_specs=[whole, whole], out_specs=whole, out...  3.41 us

profile of v6, /device:TPU:1, one launch (start us, length us, event | category | flops | bytes accessed | tf_op | source)
XLA Modules:
  0.0 136.1 jit_solution(11339616836368578648)
XLA Ops:
  0.0 7.5 %prepare.1 = bf16[128,3,2,32,128]{4,3,2,1,0:T(8,128)(2,1)S(1)} custom-call(s32[1]{0:T(128)} %bitcast.state_ref, bf16[8,512,256]{2,1,0:T(8,128)(2,1)} %bitcast.3, bf16[2,3,512,512]{3,2,1,0:T(8,128)(2,1)} %second_hbm.1, bf16[2,3,256,256]{3,2,1,0:T(8,128)(2,1)} %third_hbm.1), custom_call_target="tpu_custom_call" | custom-call | tf_op jit(solution)/shard_map/prepare/pallas_call | solution.py:217
  7.5 0.0 copy-start.1
  7.5 86.4 %all_to_all.10.got_ref = bf16[128,3,2,32,128]{4,3,2,1,0:T(8,128)(2,1)S(1)} all-to-all(bf16[128,3,2,32,128]{4,3,2,1,0:T(8,128)(2,1)S(1)} %prepare.1), channel_id=1, replica_groups=mesh['state'=2,'mode'=64] {'state','mode'}, dimensions={0} | all-to-all | bytes 12582912 | tf_op jit(solution)/shard_map/all_to_all | solution.py:236
  93.9 0.0 copy-done.1
  93.9 3.4 %apply_first.1 = bf16[128,2,32,128]{3,2,1,0:T(8,128)(2,1)S(1)} custom-call(bf16[2,3,512,512]{3,2,1,0:T(8,128)(2,1)S(1)} %copy-done.1, bf16[128,3,2,32,128]{4,3,2,1,0:T(8,128)(2,1)S(1)} %all_to_all.10.got_ref), custom_call_target="tpu_custom_call" | custom-call | tf_op jit(solution)/shard_map/apply_first/pallas_call | solution.py:237
  97.4 0.0 copy-start
  97.4 36.5 %all_to_all.11.got_ref = bf16[128,2,32,128]{3,2,1,0:T(8,128)(2,1)S(1)} all-to-all(bf16[128,2,32,128]{3,2,1,0:T(8,128)(2,1)S(1)} %apply_first.1), channel_id=1, replica_groups=mesh['state'=2,'mode'=64] {'state','mode'}, dimensions={0} | all-to-all | bytes 4194304 | tf_op jit(solution)/shard_map/all_to_all | solution.py:245
  133.8 0.0 copy-done
  133.8 2.2 %relax.1 = f32[8,512,256]{2,1,0:T(8,128)} custom-call(bf16[128,2,32,128]{3,2,1,0:T(8,128)(2,1)S(1)} %all_to_all.11.got_ref, bf16[8,512,256]{2,1,0:T(8,128)(2,1)S(1)} %bitcast.4), custom_call_target="tpu_custom_call" | custom-call | tf_op jit(solution)/shard_map/relax/pallas_call | solution.py:246
Async XLA Ops:
  7.5 86.5 %copy-start.1 = (bf16[2,3,512,512]{3,2,1,0:T(8,128)(2,1)S(1)}, bf16[2,3,512,512]{3,2,1,0:T(8,128)(2,1)}, u32[]{:S(2)}) copy-start(bf16[2,3,512,512]{3,2,1,0:T(8,128)(2,1)} %first_ref.1) | copy-start | bytes 9437188
  97.4 36.5 %copy-start = (bf16[1,8,512,256]{3,2,1,0:T(8,128)(2,1)S(1)}, bf16[1,8,512,256]{3,2,1,0:T(8,128)(2,1)}, u32[]{:S(2)}) copy-start(bf16[1,8,512,256]{3,2,1,0:T(8,128)(2,1)} %param.4) | copy-start | bytes 6291460
